TPU v7x, 32 devices: a whole 2x2x4 slice. The times are simulated.
32 devices in a mesh: obs: 4 (over y, x), par: 8 (over z, core).
Axes of the slice: x: 2, y: 2, z: 4, core: 2. Of those that a mesh axis runs over, the one named last changes fastest.
Arguments:
- jacobian: bfloat16 [2048, 32768], P('obs', 'par'), may hold values from -0.03125 to 0.03125
- probes: bfloat16 [32768, 256], P('par'), may hold values from -6 to 6
- coeffs: bfloat16 [256, 3, 128, 128], P('par'), may hold values from -0.3125 to 0.3125
- offsets: int32 [256, 2], P('par'), may hold values from -4 to 4
Outputs:
- ritz_basis: bfloat16 [32768, 256], P('par')
- basis_image: bfloat16 [32768, 256], P('par')
- ritz_matrix: float32 [256, 256], replicated
All inputs are finite; a program needn't handle non-finite values.
Results may differ from a plain program's by a relative error of at most 0.015.
Values may be sent and summed in bfloat16 or wider, within the bound.
A program may use at most 128 MiB of HBM per device.

v0:
```python
import jax
import jax.numpy as jnp
from jax import lax
from jax.sharding import PartitionSpec as P

BLK = 128
REACH = 4


def shifted(value, axis, by):
    count = lax.axis_size(axis)
    pairs = [(i, i + by) for i in range(count) if 0 <= i + by < count]
    return lax.ppermute(value, axis, pairs)


def extended_2(cells, sides, width):
    for axis, dim in sides:
        count = lax.axis_size(axis)
        ends = count - 1
        head = lax.slice_in_dim(cells, 0, width, axis=dim)
        tail = lax.slice_in_dim(cells, cells.shape[dim] - width, cells.shape[dim], axis=dim)
        cells = jnp.concatenate(
            [
                lax.ppermute(tail, axis, [(i, (i + 1) % count) for i in range(ends)]),
                cells,
                lax.ppermute(head, axis, [((i + 1) % count, i) for i in range(ends)]),
            ],
            axis=dim,
        )
    return cells


def block_index(offsets):
    count = offsets.shape[0]
    full_offsets = jnp.concatenate([jnp.zeros((count, 1), jnp.int32), offsets], axis=1)
    return jnp.arange(count, dtype=jnp.int32)[:, None] + REACH + full_offsets


def prior_forward(extended, coeffs, offsets):
    width = extended.shape[1]
    positions = block_index(offsets)
    padded = extended.reshape(-1, BLK, width)
    picked = padded[positions]
    result = jnp.einsum("bjrc,bjcn->brn", coeffs, picked, preferred_element_type=jnp.float32)
    return result.reshape(-1, width).astype(jnp.bfloat16)


def prior_adjoint(values, coeffs, offsets):
    width = values.shape[1]
    count = offsets.shape[0]
    positions = block_index(offsets)
    blocks = values.reshape(count, BLK, width)
    contrib = jnp.einsum("bjcr,bcn->bjrn", coeffs, blocks, preferred_element_type=jnp.float32)
    accumulated = jnp.zeros((count + 2 * REACH, BLK, width), jnp.float32).at[positions].add(contrib)
    inner = accumulated[REACH : REACH + count]
    from_upper = shifted(accumulated[:REACH].astype(jnp.bfloat16), "par", -1).astype(jnp.float32)
    from_lower = shifted(accumulated[REACH + count :].astype(jnp.bfloat16), "par", 1).astype(
        jnp.float32
    )
    inner = inner.at[count - REACH :].add(from_upper)
    inner = inner.at[:REACH].add(from_lower)
    return inner.reshape(-1, width)


def body(jacobian, probes, coeffs, offsets):
    total_par = jacobian.shape[1] * lax.axis_size("par")
    total_obs = jacobian.shape[0] * lax.axis_size("obs")
    probe_halo = extended_2(probes, (("par", 0),), REACH * BLK)
    sampled = prior_forward(probe_halo, coeffs, offsets)
    forward_part = jnp.dot(jacobian, sampled, preferred_element_type=jnp.float32)
    forward = lax.psum(forward_part, "par").astype(jnp.bfloat16)
    adjoint_part = lax.dot_general(
        jacobian, forward, (((0,), (0,)), ((), ())), preferred_element_type=jnp.float32
    )
    adjoint_cols = lax.psum_scatter(
        adjoint_part.astype(jnp.bfloat16), "obs", scatter_dimension=1, tiled=True
    )
    sample_cols = prior_adjoint(adjoint_cols, coeffs, offsets)
    range_sample = lax.all_gather(
        sample_cols.astype(jnp.bfloat16), "obs", axis=1, tiled=True
    ).astype(sample_cols.dtype)
    gram_part = jnp.dot(range_sample.T, range_sample, precision=lax.Precision.HIGHEST)
    gram_matrix = lax.psum(gram_part, "par") / total_par
    lower_factor = jnp.linalg.cholesky(gram_matrix)
    solved = lax.linalg.triangular_solve(
        lower_factor, range_sample, left_side=False, lower=True, transpose_a=True
    )
    ritz_basis = solved.astype(jnp.bfloat16)
    basis_halo = extended_2(ritz_basis, (("par", 0),), REACH * BLK)
    basis_image = prior_forward(basis_halo, coeffs, offsets)
    projected_part = jnp.dot(jacobian, basis_image, preferred_element_type=jnp.float32)
    projected = lax.psum(projected_part, "par")
    ritz_part = jnp.dot(projected.T, projected, precision=lax.Precision.HIGHEST)
    ritz_matrix = lax.psum(ritz_part.astype(jnp.bfloat16), "obs").astype(jnp.float32) / total_obs
    return (ritz_basis, basis_image, ritz_matrix)


def solution(mesh):
    return jax.shard_map(
        body,
        mesh=mesh,
        in_specs=(P("obs", "par"), P("par", None), P("par", None, None, None), P("par", None)),
        out_specs=(P("par", None), P("par", None), P()),
        check_vma=False,
    )
```

profile of v0, /device:TPU:0, one launch (start us, length us, event | category | flops | bytes accessed | tf_op | source)
XLA Modules:
  0.0 453.3 jit_solution(15713091920157657930)
XLA Ops:
  7.2 2.0 fusion.16
  9.2 3.1 collective-permute-start
  12.3 1.3 collective-permute-start.1
  14.5 3.0 collective-permute-done.1
  17.6 3.4 pad_maximum_fusion.1
  21.0 7.8 %gather_fusion = bf16[96,128,256]{2,1,0:T(8,128)(2,1)} fusion(bf16[40,128,256]{2,1,0:T(8,128)(2,1)} %bitcast.86, s32[1024]{0:T(1024)S(1)} %pad_clamp_fusion), kind=kCustom, calls=%fused_computation | custom fusion | bytes 12583296 | tf_op jit(solution)/shard_map/gather | solution.py:43
  28.8 4.2 bitcast_convert_fusion.1
  33.0 2.1 convolution_bitcast_fusion.1
  35.1 37.8 %all-reduce.12 = bf16[512,256]{0,1:T(8,128)(2,1)} all-reduce(f32[512,256]{0,1:T(8,128)} %convolution_bitcast_fusion.1), channel_id=1, replica_groups=mesh['obs'=4,'par'=8] {'par'}, use_global_device_ids=true, to_apply=%region_0.0 | all-reduce | flops 131072 | bytes 786432 | tf_op jit(solution)/shard_map/psum | solution.py:71
  72.9 4.9 %fusion = bf16[4096,256]{0,1:T(8,128)(2,1)} fusion(bf16[512,4096]{1,0:T(8,128)(2,1)} %param.8, bf16[512,256]{0,1:T(8,128)(2,1)} %all-reduce.12), kind=kOutput, calls=%fused_computation.6 | convolution fusion | flops 1074790400 | bytes 6553600 | tf_op jit(solution)/shard_map/dot_general | solution.py:72
  77.8 33.5 %reduce-scatter.2.cloned.1.call-done = bf16[4096,64]{0,1:T(8,128)(2,1)} async-done(((bf16[4096,256]{0,1:T(8,128)(2,1)}), bf16[4096,64]{0,1:T(8,128)(2,1)}) %reduce-scatter.2.cloned.1.call-update) | async-done | bytes 524304 | tf_op jit(solution)/shard_map/reduce_scatter | solution.py:75
  111.3 1.1 copy.28
  112.5 2.4 fusion.3
  114.8 1.2 broadcast_in_dim.5
  116.0 15.1 %scatter_fusion = f32[40,128,64]{1,2,0:T(8,128)} fusion(f32[40,128,64]{1,2,0:T(8,128)} %broadcast_in_dim.5, s32[96]{0:T(128)S(1)} %reshape.143, f32[96,128,64]{1,2,0:T(8,128)} %bitcast.88), kind=kCustom, calls=%fused_computation.2 | custom fusion | flops 786432 | bytes 9437568 | tf_op jit(solution)/shard_map/scatter-add | solution.py:54
  131.2 1.5 convert.11
  132.7 1.3 collective-permute-start.2
  134.1 3.0 collective-permute-start.3
  139.0 37.6 %all-gather.2.cloned.1.call-done = bf16[4096,256]{0,1:T(8,128)(2,1)} async-done(((bf16[4096,64]{0,1:T(8,128)(2,1)}), bf16[4096,256]{0,1:T(8,128)(2,1)}) %all-gather.2.cloned.1.call-update) | async-done | bytes 2097168 | tf_op jit(solution)/shard_map/all_gather | solution.py:79
  176.6 3.7 fusion.19
  180.5 55.3 %all-reduce.7.cloned.1.call-done = f32[256,256]{0,1:T(8,128)} async-done(((f32[256,256]{0,1:T(8,128)}), f32[256,256]{0,1:T(8,128)}) %all-reduce.7.cloned.1.call-update) | async-done | bytes 262160 | tf_op jit(solution)/shard_map/psum | solution.py:83
  235.8 1.7 broadcast_multiply_fusion
  240.3 11.7 %cholesky.50 = f32[128,128]{1,0:T(8,128)S(1)} custom-call(f32[128,128]{1,0:T(8,128)S(1)} %cholesky.118), custom_call_target="Cholesky" | custom-call | tf_op jit(solution)/shard_map/jit(cholesky)/cholesky | solution.py:84
  252.1 9.8 %custom-call.14 = f32[1,128,128]{1,2,0:T(8,128)S(1)} custom-call(f32[1,128,128]{2,1,0:T(8,128)S(1)} %get-tuple-element.60), custom_call_target="InvertDiagBlocksLowerTriangular" | custom-call | tf_op jit(solution)/shard_map/jit(cholesky)/cholesky | solution.py:84
  262.9 1.1 convolution_subtract_fusion.1
  264.0 11.7 %cholesky.105 = f32[128,128]{1,0:T(8,128)S(1)} custom-call(f32[128,128]{1,0:T(8,128)S(1)} %convolution_subtract_fusion.1), custom_call_target="Cholesky" | custom-call | tf_op jit(solution)/shard_map/jit(cholesky)/cholesky | solution.py:84
  278.8 5.5 %while.3 = (s32[]{:T(128)}, f32[256,256]{1,0:T(8,128)S(1)}, s32[2,2]{1,0:T(2,128)S(1)}, f32[2,128,128]{2,1,0:T(8,128)}, s32[]{:T(128)}) while((s32[]{:T(128)}, f32[256,256]{1,0:T(8,128)S(1)}, s32[2,2]{1,0:T(2,128)S(1)}, f32[2,128,128]{2,1,0:T(8,128)}, s32[]{:T(128)}) %tuple.41), condition=%wide.while_cond.2, body=%wide.while_body.2.sunk | while | flops 2 | bytes 132205 | solution.py:85
  279.6 2.0 bitcast_dynamic-update-slice_fusion.2
  282.2 2.0 bitcast_dynamic-update-slice_fusion.2
  284.3 20.5 %custom-call.15 = f32[2,128,128]{1,2,0:T(8,128)S(1)} custom-call(f32[2,128,128]{2,1,0:T(8,128)} %get-tuple-element.34), custom_call_target="InvertDiagBlocksLowerTriangular" | custom-call | tf_op jit(solution)/shard_map/triangular_solve | solution.py:85
  304.8 2.4 fusion.18
  307.2 2.1 convolution_subtract_fusion
  309.3 2.0 convolution_convert_fusion.1
  311.3 1.3 collective-permute-start.4
  312.7 1.3 collective-permute-start.5
  314.0 2.9 collective-permute-done.5
  316.9 3.7 pad_maximum_fusion.2
  320.6 4.4 copy.26
  325.0 7.8 %gather_fusion.1 = bf16[96,128,256]{2,1,0:T(8,128)(2,1)} fusion(bf16[40,128,256]{2,1,0:T(8,128)(2,1)} %bitcast.87, s32[1024]{0:T(1024)S(1)} %pad_clamp_fusion), kind=kCustom, calls=%fused_computation.1 | custom fusion | bytes 12583296 | tf_op jit(solution)/shard_map/gather | solution.py:43
  332.7 4.2 bitcast_convert_fusion
  337.0 1.3 copy-done.5
  338.3 2.1 convolution_bitcast_fusion
  340.4 60.1 %all-reduce.9.cloned.1.call-done = f32[512,256]{0,1:T(8,128)} async-done(((f32[512,256]{0,1:T(8,128)}), f32[512,256]{0,1:T(8,128)}) %all-reduce.9.cloned.1.call-update) | async-done | bytes 524304 | tf_op jit(solution)/shard_map/psum | solution.py:92
  400.5 2.5 convolution_convert_fusion.2
  403.0 3.1 pad_maximum_fusion
  406.1 4.1 copy.19
  410.2 34.9 %all-reduce.11.cloned.1.call-done = bf16[256,256]{1,0:T(8,128)(2,1)} async-done(((bf16[256,256]{1,0:T(8,128)(2,1)}), bf16[256,256]{1,0:T(8,128)(2,1)}) %all-reduce.11.cloned.1.call-update) | async-done | bytes 131088 | tf_op jit(solution)/shard_map/psum | solution.py:94
  445.1 1.6 convert_multiply_fusion
  (60 shorter events, 10.1 us)
Async XLA Ops:
  7.2 21.6 %copy-start = (bf16[32,3,128,128]{3,2,1,0:T(8,128)(2,1)S(1)}, bf16[32,3,128,128]{3,2,1,0:T(8,128)(2,1)}, u32[]{:S(2)}) copy-start(bf16[32,3,128,128]{3,2,1,0:T(8,128)(2,1)} %param.10) | copy-start | bytes 9437188
  7.2 104.1 %reduce-scatter.2.cloned.1.call-start = ((), (), s32[]{:S(2)}) async-start(), calls=%async_computation.1 | async-start | bytes 2621440 | tf_op jit(solution)/shard_map/reduce_scatter | solution.py:75
  9.2 5.3 %collective-permute-start = (bf16[512,256]{1,0:T(8,128)(2,1)}, bf16[512,256]{1,0:T(8,128)(2,1)}, u32[]{:S(2)}, u32[]{:S(2)}) collective-permute-start(bf16[512,256]{1,0:T(8,128)(2,1)} %get-tuple-element.53), channel_id=1, source_target_pairs={{0,1},{1,2},{2,3},{3,4},{4,5},{5,6},{6,7},{8,9},{9,10},{10,11},{11... | collective-permute-start | bytes 786440 | tf_op jit(solution)/shard_map/ppermute | solution.py:24
  12.3 5.3 %collective-permute-start.1 = (bf16[512,256]{1,0:T(8,128)(2,1)}, bf16[512,256]{1,0:T(8,128)(2,1)}, u32[]{:S(2)}, u32[]{:S(2)}) collective-permute-start(bf16[512,256]{1,0:T(8,128)(2,1)} %get-tuple-element.54), channel_id=1, source_target_pairs={{1,0},{2,1},{3,2},{4,3},{5,4},{6,5},{7,6},{9,8},{10,9},{11,10},{12... | collective-permute-start | bytes 786440 | tf_op jit(solution)/shard_map/ppermute | solution.py:26
  28.8 4.2 copy-start.8
  77.8 98.8 %all-gather.2.cloned.1.call-start = ((), (), s32[]{:S(2)}) async-start(), calls=%async_computation.2 | async-start | bytes 2621440 | tf_op jit(solution)/shard_map/all_gather | solution.py:79
  131.2 2.9 copy-start.1
  132.7 4.4 collective-permute-start.2
  134.1 3.9 collective-permute-start.3
  138.9 96.9 %all-reduce.7.cloned.1.call-start = ((), (), s32[]{:S(2)}) async-start(), calls=%async_computation.3 | async-start | bytes 524288 | tf_op jit(solution)/shard_map/psum | solution.py:83
  180.3 220.2 %all-reduce.9.cloned.1.call-start = ((), (), s32[]{:S(2)}) async-start(), calls=%async_computation.4 | async-start | bytes 1048576 | tf_op jit(solution)/shard_map/psum | solution.py:92
  239.6 0.7 copy-start.7
  275.8 1.9 copy-start.6
  304.7 2.4 copy-start.2
  307.2 9.7 %copy-start.4 = (bf16[4096,128]{0,1:T(8,128)(2,1)}, bf16[4096,128]{0,1:T(8,128)(2,1)S(1)}, u32[]{:S(2)}) copy-start(bf16[4096,128]{0,1:T(8,128)(2,1)S(1)} %get-tuple-element.63) | copy-start | bytes 3145732
  311.3 5.6 %copy-start.3 = (bf16[4096,128]{0,1:T(8,128)(2,1)}, bf16[4096,128]{0,1:T(8,128)(2,1)S(1)}, u32[]{:S(2)}) copy-start(bf16[4096,128]{0,1:T(8,128)(2,1)S(1)} %convolution_convert_fusion.1) | copy-start | bytes 3145732
  311.3 2.6 collective-permute-start.4
  312.7 4.2 collective-permute-start.5
  332.7 5.5 %copy-start.9 = (bf16[512,4096]{1,0:T(8,128)(2,1)S(1)}, bf16[512,4096]{1,0:T(8,128)(2,1)}, u32[]{:S(2)}) copy-start(bf16[512,4096]{1,0:T(8,128)(2,1)} %param.8) | copy-start | bytes 12582916
  336.9 1.3 copy-start.5
  340.4 104.7 %all-reduce.11.cloned.1.call-start = ((), (), s32[]{:S(2)}) async-start(), calls=%async_computation.5 | async-start | bytes 262144 | tf_op jit(solution)/shard_map/psum | solution.py:94
Sparse Core Ops, SparseCore 0:
  77.9 33.3 reduce-scatter.1
  139.1 37.4 all-gather.1
  180.4 55.4 all-reduce.6
  340.5 59.9 all-reduce.8
  403.8 41.2 all-reduce.10
where the time goes:
time: 454 us; the launch traced here: 453 us
  waiting for transfers between devices  228 us (50%)
  other arithmetic  88.2 us (19%)
  blocking collectives  37.8 us (8%)
  local copies, waits for them, and re-layouts  37.1 us (8%)
  matrix products  34.6 us (8%)
  between operations  15.3 us (3%)
  starting transfers between devices  11.7 us (3%)
    psum x1, waiting for transfers between devices, body(): projected = lax.psum(projected_part, 'par')  60.1 us
    psum x1, waiting for transfers between devices, body(): gram_matrix = lax.psum(gram_part, 'par') / total_par  55.3 us
    psum x1, blocking collectives, body(): forward = lax.psum(forward_part, 'par').astype(jnp.bfloat16)  37.8 us
    all_gather x1, waiting for transfers between devices, body(): lax.all_gather(sample_cols.astype(jnp.bfloat16), 'obs', axis=1, tiled=True)  37.6 us
    psum x1, waiting for transfers between devices, body(): lax.psum(ritz_part.astype(jnp.bfloat16), 'obs').astype(jnp.float32)  34.9 us
    another operation x6, other arithmetic, body(): lower_factor = jnp.linalg.cholesky(gram_matrix)  34 us
    reduce_scatter x1, waiting for transfers between devices, body(): lax.psum_scatter(adjoint_part.astype(jnp.bfloat16), 'obs', scatter_dimens...  33.5 us
    another operation x5, other arithmetic, body(): lax.linalg.triangular_solve(lower_factor, range_sample, left_side=False,...  24.6 us
  transfers between devices with their start and end apart: 11, of which 8 were waited for; matrix products, arithmetic and copies ran while one was open for 2% of the time, Pallas kernels for 0%

commit v1 on v0

--- a/solution.py
+++ b/solution.py
@@ -89,7 +89,11 @@
     basis_halo = extended_2(ritz_basis, (("par", 0),), REACH * BLK)
     basis_image = prior_forward(basis_halo, coeffs, offsets)
     projected_part = jnp.dot(jacobian, basis_image, preferred_element_type=jnp.float32)
-    projected = lax.psum(projected_part, "par")
+    projected = projected_part
+    for hop in (1, 2, 4):
+        projected = projected + lax.ppermute(
+            projected, "par", [(dev, dev ^ hop) for dev in range(8)]
+        )
     ritz_part = jnp.dot(projected.T, projected, precision=lax.Precision.HIGHEST)
     ritz_matrix = lax.psum(ritz_part.astype(jnp.bfloat16), "obs").astype(jnp.float32) / total_obs
     return (ritz_basis, basis_image, ritz_matrix)

time: 454 us -> 436 us (0.960)
  waiting for transfers between devices: 228 us -> 206 us
  starting transfers between devices: 11.7 us -> 19.5 us
    psum x1 -> x0, waiting for transfers between devices: 60.1 us -> none  [body(): projected = lax.psum(projected_part, 'par')]
    ppermute x0 -> x3, waiting for transfers between devices: none -> 38.3 us  [body(): lax.ppermute(projected, 'par', [(dev, dev ^ hop) for dev in range(8)])]
    ppermute x0 -> x3, starting transfers between devices: none -> 7.86 us  [body(): lax.ppermute(projected, 'par', [(dev, dev ^ hop) for dev in range(8)])]
  transfers between devices with their start and end apart: 11 -> 13, of which waited for: 8 -> 10; matrix products, arithmetic and copies ran while one was open for 2% -> 2% of each run, Pallas kernels for 0% -> 0%
where the time goes in v1:
time: 436 us; the launch traced here: 435 us
  waiting for transfers between devices  206 us (47%)
  other arithmetic  88.3 us (20%)
  blocking collectives  37.8 us (9%)
  local copies, waits for them, and re-layouts  35.6 us (8%)
  matrix products  32.6 us (7%)
  starting transfers between devices  19.5 us (4%)
  between operations  15.3 us (4%)
    psum x1, waiting for transfers between devices, body(): gram_matrix = lax.psum(gram_part, 'par') / total_par  55.3 us
    ppermute x3, waiting for transfers between devices, body(): lax.ppermute(projected, 'par', [(dev, dev ^ hop) for dev in range(8)])  38.3 us
    psum x1, blocking collectives, body(): forward = lax.psum(forward_part, 'par').astype(jnp.bfloat16)  37.8 us
    all_gather x1, waiting for transfers between devices, body(): lax.all_gather(sample_cols.astype(jnp.bfloat16), 'obs', axis=1, tiled=True)  37.6 us
    psum x1, waiting for transfers between devices, body(): lax.psum(ritz_part.astype(jnp.bfloat16), 'obs').astype(jnp.float32)  34.1 us
    another operation x6, other arithmetic, body(): lower_factor = jnp.linalg.cholesky(gram_matrix)  34 us
    reduce_scatter x1, waiting for transfers between devices, body(): lax.psum_scatter(adjoint_part.astype(jnp.bfloat16), 'obs', scatter_dimens...  33.5 us
    another operation x5, other arithmetic, body(): lax.linalg.triangular_solve(lower_factor, range_sample, left_side=False,...  24.6 us
  transfers between devices with their start and end apart: 13, of which 10 were waited for; matrix products, arithmetic and copies ran while one was open for 2% of the time, Pallas kernels for 0%

profile of v1, /device:TPU:0, one launch (start us, length us, event | category | flops | bytes accessed | tf_op | source)
XLA Modules:
  0.0 435.0 jit_solution(10763879777574105380)
XLA Ops:
  7.2 2.0 fusion.17
  9.2 3.1 collective-permute-start
  14.5 3.0 collective-permute-done.1
  17.6 3.4 pad_maximum_fusion.1
  21.0 7.7 %gather_fusion = bf16[96,128,256]{2,1,0:T(8,128)(2,1)} fusion(bf16[40,128,256]{2,1,0:T(8,128)(2,1)} %bitcast.84, s32[1024]{0:T(1024)S(1)} %pad_clamp_fusion), kind=kCustom, calls=%fused_computation | custom fusion | bytes 12583296 | tf_op jit(solution)/shard_map/gather | solution.py:43
  28.7 4.2 bitcast_convert_fusion.1
  32.9 2.1 convolution_bitcast_fusion.1
  35.0 37.8 %all-reduce.9 = bf16[512,256]{0,1:T(8,128)(2,1)} all-reduce(f32[512,256]{0,1:T(8,128)} %convolution_bitcast_fusion.1), channel_id=1, replica_groups=mesh['obs'=4,'par'=8] {'par'}, use_global_device_ids=true, to_apply=%region_0.0 | all-reduce | flops 131072 | bytes 786432 | tf_op jit(solution)/shard_map/psum | solution.py:71
  72.8 4.9 %fusion = bf16[4096,256]{0,1:T(8,128)(2,1)} fusion(bf16[512,4096]{1,0:T(8,128)(2,1)} %param.8, bf16[512,256]{0,1:T(8,128)(2,1)} %all-reduce.9), kind=kOutput, calls=%fused_computation.6 | convolution fusion | flops 1074790400 | bytes 6553600 | tf_op jit(solution)/shard_map/dot_general | solution.py:72
  77.8 33.5 %reduce-scatter.2.cloned.1.call-done = bf16[4096,64]{0,1:T(8,128)(2,1)} async-done(((bf16[4096,256]{0,1:T(8,128)(2,1)}), bf16[4096,64]{0,1:T(8,128)(2,1)}) %reduce-scatter.2.cloned.1.call-update) | async-done | bytes 524304 | tf_op jit(solution)/shard_map/reduce_scatter | solution.py:75
  112.4 2.4 fusion.3
  116.0 15.1 %scatter_fusion = f32[40,128,64]{1,2,0:T(8,128)} fusion(f32[40,128,64]{1,2,0:T(8,128)} %broadcast_in_dim.5, s32[96]{0:T(128)S(1)} %reshape.143, f32[96,128,64]{1,2,0:T(8,128)} %bitcast.86), kind=kCustom, calls=%fused_computation.2 | custom fusion | flops 786432 | bytes 9437568 | tf_op jit(solution)/shard_map/scatter-add | solution.py:54
  131.1 1.5 convert.11
  132.7 1.3 collective-permute-start.2
  134.1 3.0 collective-permute-start.3
  139.0 37.6 %all-gather.2.cloned.1.call-done = bf16[4096,256]{0,1:T(8,128)(2,1)} async-done(((bf16[4096,64]{0,1:T(8,128)(2,1)}), bf16[4096,256]{0,1:T(8,128)(2,1)}) %all-gather.2.cloned.1.call-update) | async-done | bytes 2097168 | tf_op jit(solution)/shard_map/all_gather | solution.py:79
  176.5 3.7 fusion.20
  180.5 55.3 %all-reduce.6.cloned.1.call-done = f32[256,256]{0,1:T(8,128)} async-done(((f32[256,256]{0,1:T(8,128)}), f32[256,256]{0,1:T(8,128)}) %all-reduce.6.cloned.1.call-update) | async-done | bytes 262160 | tf_op jit(solution)/shard_map/psum | solution.py:83
  235.8 1.7 broadcast_multiply_fusion
  240.3 11.7 %cholesky.50 = f32[128,128]{1,0:T(8,128)S(1)} custom-call(f32[128,128]{1,0:T(8,128)S(1)} %cholesky.118), custom_call_target="Cholesky" | custom-call | tf_op jit(solution)/shard_map/jit(cholesky)/cholesky | solution.py:84
  252.0 9.8 %custom-call.14 = f32[1,128,128]{1,2,0:T(8,128)S(1)} custom-call(f32[1,128,128]{2,1,0:T(8,128)S(1)} %get-tuple-element.60), custom_call_target="InvertDiagBlocksLowerTriangular" | custom-call | tf_op jit(solution)/shard_map/jit(cholesky)/cholesky | solution.py:84
  264.0 11.7 %cholesky.105 = f32[128,128]{1,0:T(8,128)S(1)} custom-call(f32[128,128]{1,0:T(8,128)S(1)} %convolution_subtract_fusion.1), custom_call_target="Cholesky" | custom-call | tf_op jit(solution)/shard_map/jit(cholesky)/cholesky | solution.py:84
  278.7 5.3 %while.3 = (s32[]{:T(128)}, f32[256,256]{1,0:T(8,128)S(1)}, s32[2,2]{1,0:T(2,128)S(1)}, f32[2,128,128]{2,1,0:T(8,128)}, s32[]{:T(128)}) while((s32[]{:T(128)}, f32[256,256]{1,0:T(8,128)S(1)}, s32[2,2]{1,0:T(2,128)S(1)}, f32[2,128,128]{2,1,0:T(8,128)}, s32[]{:T(128)}) %tuple.41), condition=%wide.while_cond.2, body=%wide.while_body.2.sunk | while | flops 2 | bytes 132205 | solution.py:85
  279.4 2.0 bitcast_dynamic-update-slice_fusion.2
  282.0 2.0 bitcast_dynamic-update-slice_fusion.2
  284.0 20.5 %custom-call.15 = f32[2,128,128]{1,2,0:T(8,128)S(1)} custom-call(f32[2,128,128]{2,1,0:T(8,128)} %get-tuple-element.34), custom_call_target="InvertDiagBlocksLowerTriangular" | custom-call | tf_op jit(solution)/shard_map/triangular_solve | solution.py:85
  304.5 2.4 fusion.19
  306.9 2.1 convolution_subtract_fusion
  309.0 2.0 convolution_convert_fusion.1
  311.1 1.3 collective-permute-start.4
  312.4 1.3 collective-permute-start.5
  313.7 2.9 collective-permute-done.5
  316.6 3.7 pad_maximum_fusion.2
  320.3 4.4 %copy.26 = bf16[5120,256]{1,0:T(8,128)(2,1)} copy(bf16[5120,256]{0,1:T(8,128)(2,1)} %pad_maximum_fusion.2) | data formatting | bytes 5242880 | tf_op jit(solution)/shard_map/reshape | solution.py:42
  324.7 7.7 %gather_fusion.1 = bf16[96,128,256]{2,1,0:T(8,128)(2,1)} fusion(bf16[40,128,256]{2,1,0:T(8,128)(2,1)} %bitcast.85, s32[1024]{0:T(1024)S(1)} %pad_clamp_fusion), kind=kCustom, calls=%fused_computation.1 | custom fusion | bytes 12583296 | tf_op jit(solution)/shard_map/gather | solution.py:43
  332.4 4.2 bitcast_convert_fusion
  336.6 1.3 convolution_bitcast_fusion
  337.9 4.8 %collective-permute-start.6 = (f32[512,256]{0,1:T(8,128)S(1)}, f32[512,256]{0,1:T(8,128)S(1)}, u32[]{:S(2)}, u32[]{:S(2)}) collective-permute-start(f32[512,256]{0,1:T(8,128)S(1)} %convolution_bitcast_fusion), channel_id=1, source_target_pairs={{0,1},{1,0},{2,3},{3,2},{4,5},{5,4},{6,7},{7,6},{8,9},{9,8},{10,11... | collective-permute-start | bytes 1572872 | tf_op jit(solution)/shard_map/ppermute | solution.py:94
  342.8 1.5 collective-permute-done.6
  344.4 1.6 collective-permute-start.7
  345.9 12.7 %collective-permute-done.7 = f32[512,256]{0,1:T(8,128)S(1)} collective-permute-done((f32[512,256]{0,1:T(8,128)S(1)}, f32[512,256]{0,1:T(8,128)S(1)}, u32[]{:S(2)}, u32[]{:S(2)}) %collective-permute-start.7) | collective-permute-done | bytes 524320 | tf_op jit(solution)/shard_map/ppermute | solution.py:94
  358.7 1.5 collective-permute-start.8
  360.2 24.1 %collective-permute-done.8 = f32[512,256]{0,1:T(8,128)S(1)} collective-permute-done((f32[512,256]{0,1:T(8,128)S(1)}, f32[512,256]{0,1:T(8,128)S(1)}, u32[]{:S(2)}, u32[]{:S(2)}) %collective-permute-start.8) | collective-permute-done | bytes 524320 | tf_op jit(solution)/shard_map/ppermute | solution.py:94
  384.3 1.3 convolution_convert_fusion.2
  385.6 3.1 pad_maximum_fusion
  388.7 4.1 copy.19
  392.8 34.1 %all-reduce.8.cloned.1.call-done = bf16[256,256]{1,0:T(8,128)(2,1)} async-done(((bf16[256,256]{1,0:T(8,128)(2,1)}), bf16[256,256]{1,0:T(8,128)(2,1)}) %all-reduce.8.cloned.1.call-update) | async-done | bytes 131088 | tf_op jit(solution)/shard_map/psum | solution.py:98
  426.9 1.6 convert_multiply_fusion
  (65 shorter events, 14.9 us)
Async XLA Ops:
  7.2 21.6 %copy-start = (bf16[32,3,128,128]{3,2,1,0:T(8,128)(2,1)S(1)}, bf16[32,3,128,128]{3,2,1,0:T(8,128)(2,1)}, u32[]{:S(2)}) copy-start(bf16[32,3,128,128]{3,2,1,0:T(8,128)(2,1)} %param.10) | copy-start | bytes 9437188
  7.2 104.1 %reduce-scatter.2.cloned.1.call-start = ((), (), s32[]{:S(2)}) async-start(), calls=%async_computation.1 | async-start | bytes 2621440 | tf_op jit(solution)/shard_map/reduce_scatter | solution.py:75
  9.2 5.3 %collective-permute-start = (bf16[512,256]{1,0:T(8,128)(2,1)}, bf16[512,256]{1,0:T(8,128)(2,1)}, u32[]{:S(2)}, u32[]{:S(2)}) collective-permute-start(bf16[512,256]{1,0:T(8,128)(2,1)} %get-tuple-element.53), channel_id=1, source_target_pairs={{0,1},{1,2},{2,3},{3,4},{4,5},{5,6},{6,7},{8,9},{9,10},{10,11},{11... | collective-permute-start | bytes 786440 | tf_op jit(solution)/shard_map/ppermute | solution.py:24
  12.3 5.2 %collective-permute-start.1 = (bf16[512,256]{1,0:T(8,128)(2,1)}, bf16[512,256]{1,0:T(8,128)(2,1)}, u32[]{:S(2)}, u32[]{:S(2)}) collective-permute-start(bf16[512,256]{1,0:T(8,128)(2,1)} %get-tuple-element.54), channel_id=1, source_target_pairs={{1,0},{2,1},{3,2},{4,3},{5,4},{6,5},{7,6},{9,8},{10,9},{11,10},{12... | collective-permute-start | bytes 786440 | tf_op jit(solution)/shard_map/ppermute | solution.py:26
  28.7 4.2 copy-start.8
  77.7 98.8 %all-gather.2.cloned.1.call-start = ((), (), s32[]{:S(2)}) async-start(), calls=%async_computation.2 | async-start | bytes 2621440 | tf_op jit(solution)/shard_map/all_gather | solution.py:79
  131.1 2.9 copy-start.1
  132.7 4.4 %collective-permute-start.2 = (bf16[4,128,64]{1,2,0:T(8,128)(2,1)S(1)}, bf16[4,128,64]{1,2,0:T(8,128)(2,1)S(1)}, u32[]{:S(2)}, u32[]{:S(2)}) collective-permute-start(bf16[4,128,64]{1,2,0:T(8,128)(2,1)S(1)} %get-tuple-element.56), channel_id=1, source_target_pairs={{1,0},{2,1},{3,2},{4,3},{5,4},{6,5},{7,6},{9,8},{10,9},{11,10},{12... | collective-permute-start | bytes 196616 | tf_op jit(solution)/shard_map/ppermute | solution.py:13
  134.1 3.9 collective-permute-start.3
  138.9 96.9 %all-reduce.6.cloned.1.call-start = ((), (), s32[]{:S(2)}) async-start(), calls=%async_computation.3 | async-start | bytes 524288 | tf_op jit(solution)/shard_map/psum | solution.py:83
  180.2 246.6 %all-reduce.8.cloned.1.call-start = ((), (), s32[]{:S(2)}) async-start(), calls=%async_computation.4 | async-start | bytes 262144 | tf_op jit(solution)/shard_map/psum | solution.py:98
  239.6 0.7 copy-start.7
  275.8 1.8 copy-start.6
  304.5 2.4 copy-start.2
  306.9 9.7 %copy-start.4 = (bf16[4096,128]{0,1:T(8,128)(2,1)}, bf16[4096,128]{0,1:T(8,128)(2,1)S(1)}, u32[]{:S(2)}) copy-start(bf16[4096,128]{0,1:T(8,128)(2,1)S(1)} %get-tuple-element.63) | copy-start | bytes 3145732
  311.0 5.6 %copy-start.3 = (bf16[4096,128]{0,1:T(8,128)(2,1)}, bf16[4096,128]{0,1:T(8,128)(2,1)S(1)}, u32[]{:S(2)}) copy-start(bf16[4096,128]{0,1:T(8,128)(2,1)S(1)} %convolution_convert_fusion.1) | copy-start | bytes 3145732
  311.1 2.6 collective-permute-start.4
  312.4 4.2 collective-permute-start.5
  332.4 4.2 copy-start.9
  336.6 1.3 copy-start.5
  337.9 6.4 %collective-permute-start.6 = (f32[512,256]{0,1:T(8,128)S(1)}, f32[512,256]{0,1:T(8,128)S(1)}, u32[]{:S(2)}, u32[]{:S(2)}) collective-permute-start(f32[512,256]{0,1:T(8,128)S(1)} %convolution_bitcast_fusion), channel_id=1, source_target_pairs={{0,1},{1,0},{2,3},{3,2},{4,5},{5,4},{6,7},{7,6},{8,9},{9,8},{10,11... | collective-permute-start | bytes 1572872 | tf_op jit(solution)/shard_map/ppermute | solution.py:94
  344.4 14.3 %collective-permute-start.7 = (f32[512,256]{0,1:T(8,128)S(1)}, f32[512,256]{0,1:T(8,128)S(1)}, u32[]{:S(2)}, u32[]{:S(2)}) collective-permute-start(f32[512,256]{0,1:T(8,128)S(1)} %add.95), channel_id=1, source_target_pairs={{0,2},{1,3},{2,0},{3,1},{4,6},{5,7},{6,4},{7,5},{8,10},{9,11},{10,... | collective-permute-start | bytes 1572872 | tf_op jit(solution)/shard_map/ppermute | solution.py:94
  358.7 25.5 %collective-permute-start.8 = (f32[512,256]{0,1:T(8,128)S(1)}, f32[512,256]{0,1:T(8,128)S(1)}, u32[]{:S(2)}, u32[]{:S(2)}) collective-permute-start(f32[512,256]{0,1:T(8,128)S(1)} %add.96), channel_id=1, source_target_pairs={{0,4},{1,5},{2,6},{3,7},{4,0},{5,1},{6,2},{7,3},{8,12},{9,13},{10,... | collective-permute-start | bytes 1572872 | tf_op jit(solution)/shard_map/ppermute | solution.py:94
Sparse Core Ops, SparseCore 0:
  77.8 33.3 reduce-scatter.1
  139.0 37.4 all-gather.1
  180.4 55.4 all-reduce.5
  385.7 41.0 all-reduce.7
